TPU v7x, 512 devices: a whole 4x8x8 slice. The times are simulated.
512 devices in a mesh: seq: 8 (over y_lo, x), fsdp: 64 (over z, y_hi, core).
Axes of the slice: x: 4, y: 8 (y_hi: 4, y_lo: 2; y = y_hi * 2 + y_lo), z: 8, core: 2. Of those that a mesh axis runs over, the one named last changes fastest.
Arguments:
- hidden: bfloat16 [2048, 8192], P('seq', 'fsdp'), may hold values from -28 to 28
- q_weight: bfloat16 [8192, 8192], P('fsdp'), may hold values from -0.0625 to 0.0625
- kv_weight: bfloat16 [2048, 8192], P(None, 'fsdp'), may hold values from -0.0625 to 0.0625
- d_attended: bfloat16 [2048, 8192], P('seq', 'fsdp'), may hold values from -6 to 6
- doc_lengths: int32 [4], replicated, may hold values from 1 to 1536, as said below
- prompt_pos: int32 [128], replicated, may hold values from 0 to 2047, as said below
Outputs:
- attended: bfloat16 [2048, 8192], P('seq', 'fsdp')
- prompt_grad: float32 [128, 8192], P('seq', 'fsdp')
Inputs may be any that keep to these rules, and one draw needn't show every extreme that they name: `doc_lengths`: 4 document lengths in pack order that sum to 2048; exactly one is 1536, at a position that varies from draw to draw, and the others are at least 1. `prompt_pos`: for every block i of 256 rows, entries i * 16 to (i + 1) * 16 - 1 are distinct rows of that block in rising order; row 0 and row 2047 are always among them.
All inputs are finite; a program needn't handle non-finite values.
Results may differ from a plain program's by a relative error of at most 0.017.
The roundings to bfloat16 on the way count: a program that leaves them out, or rounds other values in their place, can miss the bound.
Values may be sent and summed in bfloat16 or wider, within the bound.
A program may use at most 64 MiB of HBM per device.

v0:
```python
import math
import jax
import jax.numpy as jnp
from jax import lax
from jax.sharding import PartitionSpec as P

GROUP = 8
rope_theta = 1000000.0


def locate(tokens, doc_lengths):
    doc_ends = jnp.cumsum(doc_lengths)
    segment = jnp.sum((tokens[:, None] >= doc_ends[None, :]).astype(jnp.int32), axis=1)
    doc_starts = doc_ends - doc_lengths
    picked = segment[:, None] == jnp.arange(doc_lengths.shape[0], dtype=jnp.int32)[None, :]
    opening = jnp.sum(jnp.where(picked, doc_starts[None, :], 0), axis=1)
    return (segment, tokens - opening)


def rotate(vectors, positions, factor):
    halfway = vectors.shape[-1] // 2
    steps_up = jnp.arange(halfway, dtype=jnp.float32)
    frequency = jnp.exp(steps_up * (-2.0 * math.log(rope_theta) / vectors.shape[-1]))
    angles = positions.astype(jnp.float32)[:, None] * frequency[None, :]
    cosine = jnp.cos(angles)
    sine_part = jnp.sin(angles)
    leading = vectors[..., :halfway]
    trailing = vectors[..., halfway:]
    return jnp.concatenate(
        [
            leading * cosine - factor * trailing * sine_part,
            trailing * cosine + factor * leading * sine_part,
        ],
        axis=-1,
    )


def per_device(hidden, q_weight, kv_weight, d_attended, doc_lengths, prompt_pos):
    seq_count = lax.axis_size("seq")
    row_count = hidden.shape[0]
    head_dim = q_weight.shape[0]
    kv_width = kv_weight.shape[0]
    seq_length = row_count * seq_count
    prompt_count = prompt_pos.shape[0]
    prompt_local = prompt_count // seq_count
    seq_rank = lax.axis_index("seq")
    fsdp_rank = lax.axis_index("fsdp")
    group_index = fsdp_rank // GROUP
    score_scale = 1.0 / math.sqrt(head_dim)
    first_row = seq_rank * row_count
    all_tokens = jnp.arange(seq_length, dtype=jnp.int32)
    segment_all, place_all = locate(all_tokens, doc_lengths)
    own_tokens = first_row + jnp.arange(row_count, dtype=jnp.int32)
    segment_own = lax.dynamic_slice_in_dim(segment_all, first_row, row_count)
    place_own = lax.dynamic_slice_in_dim(place_all, first_row, row_count)
    kv_partial = lax.dot_general(
        hidden, kv_weight, (((1,), (1,)), ((), ())), preferred_element_type=jnp.float32
    )
    kv_summed = lax.psum(kv_partial, "fsdp")
    kv_group = lax.dynamic_slice_in_dim(
        kv_summed, group_index * 2 * head_dim, 2 * head_dim, 1
    ).astype(jnp.bfloat16)
    key_own = rotate(kv_group[:, :head_dim].astype(jnp.float32), place_own, 1.0).astype(
        jnp.bfloat16
    )
    kv_block = jnp.concatenate([key_own, kv_group[:, head_dim:]], axis=1)
    kv_full = lax.all_gather(kv_block, "seq", axis=0, tiled=True)
    q_pre = lax.dot_general(
        lax.all_gather(hidden, "fsdp", axis=1, tiled=True),
        q_weight,
        (((1,), (1,)), ((), ())),
        preferred_element_type=jnp.float32,
    )
    own_query = rotate(q_pre, place_own, 1.0).astype(jnp.bfloat16)
    block_len = 512
    block_count = seq_length // block_len
    key_blocks = kv_full[:, :head_dim].reshape(block_count, block_len, head_dim)
    value_blocks = kv_full[:, head_dim:].reshape(block_count, block_len, head_dim)
    key_segments = segment_all.reshape(block_count, block_len)
    key_tokens = all_tokens.reshape(block_count, block_len)
    raw_scores = (
        jnp.einsum("tc,bkc->btk", own_query, key_blocks, preferred_element_type=jnp.float32)
        * score_scale
    )
    allowed = (key_segments[:, None, :] == segment_own[None, :, None]) & (
        key_tokens[:, None, :] <= own_tokens[None, :, None]
    )
    scores = jnp.where(allowed, raw_scores, -jnp.inf)
    row_max = jnp.max(scores, axis=(0, 2))
    exponent_terms = jnp.exp(scores - row_max[None, :, None])
    row_sum = jnp.sum(exponent_terms, axis=(0, 2))
    attention_probs = (exponent_terms / row_sum[None, :, None]).astype(jnp.bfloat16)
    attended_sum = jnp.einsum(
        "btk,bkc->tc", attention_probs, value_blocks, preferred_element_type=jnp.float32
    )
    attended = attended_sum.astype(jnp.bfloat16)
    rowdot = jnp.sum(d_attended.astype(jnp.float32) * attended.astype(jnp.float32), axis=1)
    local_prompts = (
        lax.dynamic_slice_in_dim(prompt_pos, seq_rank * prompt_local, prompt_local) - first_row
    )
    row_probs = jnp.take(attention_probs, local_prompts, axis=1)
    row_upstream = jnp.take(d_attended, local_prompts, axis=0)
    row_dprobs = jnp.einsum(
        "pc,bkc->bpk", row_upstream, value_blocks, preferred_element_type=jnp.float32
    )
    row_dot = jnp.take(rowdot, local_prompts)
    row_dscores = (row_probs.astype(jnp.float32) * (row_dprobs - row_dot[None, :, None])).astype(
        jnp.bfloat16
    )
    query_grad = (
        jnp.einsum("bpk,bkc->pc", row_dscores, key_blocks, preferred_element_type=jnp.float32)
        * score_scale
    )
    query_grad = rotate(query_grad, jnp.take(place_own, local_prompts), -1.0).astype(jnp.bfloat16)
    block_of = prompt_pos // block_len
    column_of = prompt_pos % block_len
    col_probs = attention_probs[block_of, :, column_of]
    col_values = value_blocks[block_of, column_of]
    col_dprobs = lax.dot_general(
        col_values, d_attended, (((1,), (1,)), ((), ())), preferred_element_type=jnp.float32
    )
    col_dscores = (col_probs.astype(jnp.float32) * (col_dprobs - rowdot[None, :])).astype(
        jnp.bfloat16
    )
    key_grad = jnp.dot(col_dscores, own_query, preferred_element_type=jnp.float32) * score_scale
    key_grad = rotate(key_grad, jnp.take(place_all, prompt_pos), -1.0)
    value_grad = jnp.dot(col_probs, d_attended, preferred_element_type=jnp.float32)
    kv_grad_mine = jnp.concatenate([key_grad, value_grad], axis=1)
    seq_summed = lax.psum_scatter(kv_grad_mine, "seq", scatter_dimension=0, tiled=True)
    wide_own = jnp.zeros((prompt_local, kv_width), jnp.float32)
    wide_own = lax.dynamic_update_slice_in_dim(wide_own, seq_summed, group_index * 2 * head_dim, 1)
    kv_grad = lax.psum(wide_own, "fsdp").astype(jnp.bfloat16)
    q_part = lax.psum_scatter(
        lax.dot_general(
            q_weight, query_grad, (((0,), (1,)), ((), ())), preferred_element_type=jnp.float32
        ),
        "fsdp",
        scatter_dimension=0,
        tiled=True,
    )
    kv_part = jnp.dot(kv_grad, kv_weight, preferred_element_type=jnp.float32)
    prompt_grad = q_part.T + kv_part
    return (attended, prompt_grad)


def solution(mesh):
    placed = (P("seq", "fsdp"), P("fsdp", None), P(None, "fsdp"), P("seq", "fsdp"), P(), P())
    return jax.shard_map(
        per_device,
        mesh=mesh,
        in_specs=placed,
        out_specs=(P("seq", "fsdp"), P("seq", "fsdp")),
        check_vma=False,
    )
```

profile of v0, /device:TPU:8, one launch (start us, length us, event | category | flops | bytes accessed | tf_op | source)
XLA Modules:
  0.0 729.2 jit_solution(16325572370149899096)
XLA Ops:
  7.2 0.7 all-gather.5.cloned.1.call-update
  8.0 2.8 fusion.74
  11.3 314.8 %all-reduce.2 = bf16[256,2048]{0,1:T(8,128)(2,1)S(1)} all-reduce(f32[256,2048]{0,1:T(8,128)} %fusion.74), channel_id=1, replica_groups=mesh['seq'=8,'fsdp'=64] {'fsdp'}, use_global_device_ids=true, to_apply=%region_2.3 | all-reduce | flops 524288 | bytes 3145728 | tf_op jit(solution)/shard_map/psum | solution.py:59
  326.2 3.7 fusion.75
  333.1 1.1 gather_fusion.6
  335.3 36.3 %all-gather.3.cloned.1.call-done = bf16[2048,256]{0,1:T(8,128)(2,1)} async-done(((bf16[256,256]{0,1:T(8,128)(2,1)}), bf16[2048,256]{0,1:T(8,128)(2,1)}) %all-gather.3.cloned.1.call-update) | async-done | bytes 1048592 | tf_op jit(solution)/shard_map/all_gather | solution.py:67
  371.7 2.1 fusion.72
  374.1 0.7 fusion.73
  375.6 1.8 copy.48
  377.4 1.8 gather_fusion
  379.2 2.0 copy.62
  381.3 1.1 gather_fusion.4
  382.4 2.5 gather_fusion.5
  384.9 1.4 multiply_reduce_fusion
  387.9 1.1 convolution_multiply_fusion
  389.0 0.9 fusion.38
  389.9 0.8 copy.59
  390.7 1.6 fusion.9
  392.4 1.2 convolution_bitcast_fusion
  393.7 0.7 copy.54
  394.4 39.2 %reduce-scatter.7.cloned.1.call-done = f32[16,256]{1,0:T(8,128)} async-done(((f32[128,256]{1,0:T(8,128)}), f32[16,256]{1,0:T(8,128)}) %reduce-scatter.7.cloned.1.call-update) | async-done | bytes 16400
  433.6 0.8 copy.60
  434.6 286.0 %all-reduce.3 = bf16[16,2048]{0,1:T(8,128)(2,1)} all-reduce(f32[16,2048]{0,1:T(8,128)S(1)} %constant_dynamic-update-slice_fusion), channel_id=1, replica_groups=mesh['seq'=8,'fsdp'=64] {'fsdp'}, use_global_device_ids=true, to_apply=%region_9.10 | all-reduce | flops 32768 | bytes 196608 | tf_op jit(solution)/shard_map/psum | solution.py:132
  720.5 2.1 convolution_add_fusion
  (57 shorter events, 7.7 us)
Async XLA Ops:
  7.2 319.1 %copy-start = (bf16[128,8192]{1,0:T(8,128)(2,1)S(1)}, bf16[128,8192]{1,0:T(8,128)(2,1)}, u32[]{:S(2)}) copy-start(bf16[128,8192]{1,0:T(8,128)(2,1)} %param.7) | copy-start | bytes 6291460
  7.2 3.7 copy-start.6
  7.2 319.0 %all-gather.5.cloned.1.call-start = ((), (), s32[]{:S(2)}) async-start(), calls=%async_computation.3 | async-start | bytes 4259840 | tf_op jit(solution)/shard_map/all_gather | solution.py:69
  7.9 363.7 %all-gather.3.cloned.1.call-start = ((), (), s32[]{:S(2)}) async-start(), calls=%async_computation.2 | async-start | bytes 1179648 | tf_op jit(solution)/shard_map/all_gather | solution.py:67
  326.2 5.0 copy-start.2
  326.2 5.1 copy-start.4
  331.0 102.7 %reduce-scatter.7.cloned.1.call-start = ((), (), s32[]{:S(2)}) async-start(), calls=%async_computation.5 | async-start | bytes 147456
  331.9 42.2 %copy-start.3 = (s32[16]{0:T(128)}, s32[16]{0:T(128)S(1)}, u32[]{:S(2)}) copy-start(s32[16]{0:T(128)S(1)} %get-tuple-element.13) | copy-start | bytes 196
  374.1 0.8 copy-start.1
  386.4 5.9 copy-start.5
  390.6 329.9 %reduce-scatter.5.cloned.1.call-start = ((), (), s32[]{:S(2)}) async-start(), calls=%async_computation.4 | async-start | bytes 532480 | tf_op jit(solution)/shard_map/reduce_scatter | solution.py:133
Sparse Core Ops, SparseCore 0:
  11.2 95.6 all-gather.4
  331.1 40.5 all-gather.2
  390.7 42.8 reduce-scatter.6
  438.0 139.4 reduce-scatter.4
where the time goes:
time: 730 us; the launch traced here: 729 us
  blocking collectives  601 us (82%)
  waiting for transfers between devices  76.3 us (10%)
  local copies, waits for them, and re-layouts  17.6 us (2%)
  matrix products  14.9 us (2%)
  between operations  14 us (2%)
    psum x1, blocking collectives, per_device(): kv_summed = lax.psum(kv_partial, 'fsdp')  315 us
    psum x1, blocking collectives, per_device(): kv_grad = lax.psum(wide_own, 'fsdp').astype(jnp.bfloat16)  286 us
    unnamed x5, waiting for transfers between devices  39.9 us
    all_gather x1, waiting for transfers between devices, per_device(): kv_full = lax.all_gather(kv_block, 'seq', axis=0, tiled=True)  36.3 us
  transfers between devices with their start and end apart: 4, of which 2 were waited for; matrix products, arithmetic and copies ran while one was open for 2% of the time, Pallas kernels for 0%

commit v1 on v0

--- a/solution.py
+++ b/solution.py
@@ -129,7 +129,7 @@
     seq_summed = lax.psum_scatter(kv_grad_mine, "seq", scatter_dimension=0, tiled=True)
     wide_own = jnp.zeros((prompt_local, kv_width), jnp.float32)
     wide_own = lax.dynamic_update_slice_in_dim(wide_own, seq_summed, group_index * 2 * head_dim, 1)
-    kv_grad = lax.psum(wide_own, "fsdp").astype(jnp.bfloat16)
+    kv_grad = jnp.sum(lax.all_gather(wide_own, "fsdp"), axis=0).astype(jnp.bfloat16)
     q_part = lax.psum_scatter(
         lax.dot_general(
             q_weight, query_grad, (((0,), (1,)), ((), ())), preferred_element_type=jnp.float32

time: 730 us -> 684 us (0.937)
  the two profiles are of different devices: /device:TPU:8 before, /device:TPU:2 now
where the time goes in v1:
time: 684 us; the launch traced here: 683 us
  waiting for transfers between devices  317 us (46%)
  blocking collectives  311 us (45%)
  local copies, waits for them, and re-layouts  18.4 us (3%)
  matrix products  14.4 us (2%)
  between operations  14.1 us (2%)
  other arithmetic  7.73 us (1%)
    psum x1, blocking collectives, per_device(): kv_summed = lax.psum(kv_partial, 'fsdp')  311 us
    reduce_scatter x1, waiting for transfers between devices, per_device(): lax.psum_scatter(lax.dot_general(q_weight, query_grad, (((0,), (1,)), (()...  136 us
    all_gather x1, waiting for transfers between devices, per_device(): lax.all_gather(wide_own, 'fsdp')  96.3 us
    unnamed x6, waiting for transfers between devices  43.1 us
    all_gather x1, waiting for transfers between devices, per_device(): kv_full = lax.all_gather(kv_block, 'seq', axis=0, tiled=True)  41.5 us
  transfers between devices with their start and end apart: 5, of which 4 were waited for; matrix products, arithmetic and copies ran while one was open for 3% of the time, Pallas kernels for 0%

profile of v1, /device:TPU:2, one launch (start us, length us, event | category | flops | bytes accessed | tf_op | source)
XLA Modules:
  0.0 683.1 jit_solution(801676571477464284)
XLA Ops:
  8.0 0.8 reduce-window.8
  8.8 2.8 fusion.74
  12.0 311.1 %all-reduce.1 = bf16[256,2048]{0,1:T(8,128)(2,1)S(1)} all-reduce(f32[256,2048]{0,1:T(8,128)} %fusion.74), channel_id=1, replica_groups=mesh['seq'=8,'fsdp'=64] {'fsdp'}, use_global_device_ids=true, to_apply=%region_2.3 | all-reduce | flops 524288 | bytes 3145728 | tf_op jit(solution)/shard_map/psum | solution.py:59
  323.2 3.7 fusion.75
  328.1 1.1 gather_fusion.6
  329.4 41.5 %all-gather.4.cloned.1.call-done = bf16[2048,256]{0,1:T(8,128)(2,1)} async-done(((bf16[256,256]{0,1:T(8,128)(2,1)}), bf16[2048,256]{0,1:T(8,128)(2,1)}) %all-gather.4.cloned.1.call-update) | async-done | bytes 1048592 | tf_op jit(solution)/shard_map/all_gather | solution.py:67
  370.9 2.1 fusion.72
  373.0 1.3 copy.63
  374.3 1.0 copy.65
  376.7 2.6 gather_fusion.5
  379.2 1.1 gather_fusion.4
  380.3 1.4 multiply_reduce_fusion
  382.0 1.1 convolution_multiply_fusion
  383.3 0.7 copy.61
  384.2 42.4 %reduce-scatter.7.cloned.1.call-done = f32[16,256]{1,0:T(8,128)} async-done(((f32[128,256]{1,0:T(8,128)}), f32[16,256]{1,0:T(8,128)}) %reduce-scatter.7.cloned.1.call-update) | async-done | bytes 16400
  426.5 0.8 copy.62
  430.9 1.9 copy.48
  432.7 1.8 gather_fusion
  434.6 1.6 fusion.9
  436.3 1.3 convolution_bitcast_fusion
  438.4 96.3 %all-gather.8.cloned.1.call-done = f32[64,16,2048]{2,1,0:T(8,128)} async-done(((f32[1,16,2048]{2,1,0:T(8,128)}), f32[64,16,2048]{2,1,0:T(8,128)}) %all-gather.8.cloned.1.call-update) | async-done | bytes 8388624 | tf_op jit(solution)/shard_map/all_gather | solution.py:132
  534.6 3.8 reduce_sum.49
  538.7 136.3 %reduce-scatter.5.cloned.1.call-done = f32[128,16]{0,1:T(8,128)} async-done(((f32[8192,16]{0,1:T(8,128)}), f32[128,16]{0,1:T(8,128)}) %reduce-scatter.5.cloned.1.call-update) | async-done | bytes 8208 | tf_op jit(solution)/shard_map/reduce_scatter | solution.py:133
  675.0 1.6 convolution_add_fusion
  (62 shorter events, 8.9 us)
Async XLA Ops:
  7.2 316.0 %copy-start = (bf16[128,8192]{1,0:T(8,128)(2,1)S(1)}, bf16[128,8192]{1,0:T(8,128)(2,1)}, u32[]{:S(2)}) copy-start(bf16[128,8192]{1,0:T(8,128)(2,1)} %param.7) | copy-start | bytes 6291460
  7.2 4.6 copy-start.6
  7.2 316.0 %all-gather.6.cloned.1.call-start = ((), (), s32[]{:S(2)}) async-start(), calls=%async_computation.3 | async-start | bytes 4259840 | tf_op jit(solution)/shard_map/all_gather | solution.py:69
  7.9 363.0 %all-gather.4.cloned.1.call-start = ((), (), s32[]{:S(2)}) async-start(), calls=%async_computation.2 | async-start | bytes 1179648 | tf_op jit(solution)/shard_map/all_gather | solution.py:67
  323.2 5.0 copy-start.5
  323.2 6.1 copy-start.3
  328.0 98.6 %reduce-scatter.7.cloned.1.call-start = ((), (), s32[]{:S(2)}) async-start(), calls=%async_computation.6 | async-start | bytes 147456
  374.3 1.7 copy-start.1
  384.1 150.5 %all-gather.8.cloned.1.call-start = ((), (), s32[]{:S(2)}) async-start(), calls=%async_computation.5 | async-start | bytes 8519680 | tf_op jit(solution)/shard_map/all_gather | solution.py:132
  427.4 0.7 copy-start.4
  428.1 246.8 %reduce-scatter.5.cloned.1.call-start = ((), (), s32[]{:S(2)}) async-start(), calls=%async_computation.4 | async-start | bytes 532480 | tf_op jit(solution)/shard_map/reduce_scatter | solution.py:133
  438.4 236.6 %copy-start.2 = (bf16[2048,128]{1,0:T(8,128)(2,1)S(1)}, bf16[2048,128]{1,0:T(8,128)(2,1)}, u32[]{:S(2)}) copy-start(bf16[2048,128]{1,0:T(8,128)(2,1)} %param.8) | copy-start | bytes 1572868
Sparse Core Ops, SparseCore 0:
  11.2 92.9 all-gather.5
  328.1 42.7 all-gather.3
  384.2 42.2 reduce-scatter.6
  429.7 104.8 all-gather.7
  538.9 135.9 reduce-scatter.4

commit v2 on v0

--- a/solution.py
+++ b/solution.py
@@ -64,7 +64,9 @@
         jnp.bfloat16
     )
     kv_block = jnp.concatenate([key_own, kv_group[:, head_dim:]], axis=1)
-    kv_full = lax.all_gather(kv_block, "seq", axis=0, tiled=True)
+    kv_full = jnp.concatenate(
+        lax.all_to_all(jnp.stack([kv_block] * lax.axis_size("seq")), "seq", 0, 0), axis=0
+    )
     q_pre = lax.dot_general(
         lax.all_gather(hidden, "fsdp", axis=1, tiled=True),
         q_weight,

time: 730 us -> 695 us (0.952)
  waiting for transfers between devices: 76.3 us -> 38.9 us
  starting transfers between devices: 0.16 us -> 9.14 us
    all_gather x1 -> x0, waiting for transfers between devices: 36.3 us -> none  [per_device(): kv_full = lax.all_gather(kv_block, 'seq', axis=0, tiled=True)]
    all_to_all x0 -> x1, starting transfers between devices: none -> 9.06 us  [per_device(): lax.all_to_all(jnp.stack([kv_block] * lax.axis_size('seq')), 'seq', 0, 0)]
    unnamed x5 -> x4, waiting for transfers between devices: 39.9 us -> 33.1 us
where the time goes in v2:
time: 695 us
  blocking collectives  598 us (86%)
  waiting for transfers between devices  38.9 us (6%)
  local copies, waits for them, and re-layouts  15.3 us (2%)
  matrix products  14.9 us (2%)
  between operations  14 us (2%)
  starting transfers between devices  9.14 us (1%)
    psum x1, blocking collectives, per_device(): kv_summed = lax.psum(kv_partial, 'fsdp')  312 us
    psum x1, blocking collectives, per_device(): kv_grad = lax.psum(wide_own, 'fsdp').astype(jnp.bfloat16)  286 us
    unnamed x4, waiting for transfers between devices  33.1 us
  transfers between devices with their start and end apart: 4, of which 2 were waited for; matrix products, arithmetic and copies ran while one was open for 2% of the time, Pallas kernels for 0%

profile of v2, /device:TPU:8, one launch (start us, length us, event | category | flops | bytes accessed | tf_op | source)
XLA Modules:
  0.0 694.8 jit_solution(8466334145542350254)
XLA Ops:
  7.9 2.8 fusion.74
  11.3 311.5 %all-reduce.2 = bf16[256,2048]{0,1:T(8,128)(2,1)S(1)} all-reduce(f32[256,2048]{0,1:T(8,128)} %fusion.74), channel_id=1, replica_groups=mesh['seq'=8,'fsdp'=64] {'fsdp'}, use_global_device_ids=true, to_apply=%region_2.3 | all-reduce | flops 524288 | bytes 3145728 | tf_op jit(solution)/shard_map/psum | solution.py:59
  322.9 3.7 fusion.75
  327.1 1.0 stack.2
  328.1 9.1 %all-to-all-start = ((bf16[8,256,256]{2,1,0:T(8,128)(2,1)}), bf16[8,256,256]{2,1,0:T(8,128)(2,1)S(1)}, u32[]{:S(2)}, u32[]{:S(2)}) async-start(bf16[8,256,256]{2,1,0:T(8,128)(2,1)} %stack.2), calls=%async_computation | async-start | bytes 2097152 | tf_op jit(solution)/shard_map/all_to_all | solution.py:68
  339.3 1.1 gather_fusion.6
  341.5 5.7 all-to-all-done
  347.3 0.9 fusion.72
  349.6 1.8 copy.48
  351.4 1.8 gather_fusion
  353.3 1.1 gather_fusion.4
  354.4 2.6 gather_fusion.5
  356.9 1.4 multiply_reduce_fusion
  358.4 0.8 gather_fusion.2
  360.0 1.1 convolution_multiply_fusion
  361.1 0.8 fusion.38
  361.9 0.7 copy.57
  362.7 1.6 fusion.9
  364.5 1.2 convolution_bitcast_fusion
  365.8 0.7 copy.51
  366.5 32.4 %reduce-scatter.7.cloned.1.call-done = f32[16,256]{1,0:T(8,128)} async-done(((f32[128,256]{1,0:T(8,128)}), f32[16,256]{1,0:T(8,128)}) %reduce-scatter.7.cloned.1.call-update) | async-done | bytes 16400
  398.9 0.8 copy.58
  399.8 286.3 %all-reduce.3 = bf16[16,2048]{0,1:T(8,128)(2,1)} all-reduce(f32[16,2048]{0,1:T(8,128)S(1)} %constant_dynamic-update-slice_fusion), channel_id=1, replica_groups=mesh['seq'=8,'fsdp'=64] {'fsdp'}, use_global_device_ids=true, to_apply=%region_9.10 | all-reduce | flops 32768 | bytes 196608 | tf_op jit(solution)/shard_map/psum | solution.py:134
  686.1 2.1 convolution_add_fusion
  (64 shorter events, 7.4 us)
Async XLA Ops:
  7.2 315.7 %copy-start = (bf16[128,8192]{1,0:T(8,128)(2,1)S(1)}, bf16[128,8192]{1,0:T(8,128)(2,1)}, u32[]{:S(2)}) copy-start(bf16[128,8192]{1,0:T(8,128)(2,1)} %param.7) | copy-start | bytes 6291460
  7.2 3.6 copy-start.10
  7.2 315.7 %all-gather.2.cloned.1.call-start = ((), (), s32[]{:S(2)}) async-start(), calls=%async_computation.3 | async-start | bytes 4259840 | tf_op jit(solution)/shard_map/all_gather | solution.py:71
  11.0 315.6 %copy-start.4 = (f32[64]{0:T(128)}, f32[64]{0:T(128)S(1)}, u32[]{:S(2)}) copy-start(f32[64]{0:T(128)S(1)} %multiply_exponential_fusion) | copy-start | bytes 772
  326.6 10.7 %copy-start.2 = (bf16[256,128]{1,0:T(8,128)(2,1)S(1)}, bf16[256,128]{1,0:T(8,128)(2,1)}, u32[]{:S(2)}) copy-start(bf16[256,128]{1,0:T(8,128)(2,1)} %param.9) | copy-start | bytes 196612
  326.6 10.8 %copy-start.8 = (s32[128]{0:T(128)S(1)}, s32[128]{0:T(128)}, u32[]{:S(2)}) copy-start(s32[128]{0:T(128)} %param.11) | copy-start | bytes 1540
  328.1 19.1 %all-to-all-start = ((bf16[8,256,256]{2,1,0:T(8,128)(2,1)}), bf16[8,256,256]{2,1,0:T(8,128)(2,1)S(1)}, u32[]{:S(2)}, u32[]{:S(2)}) async-start(bf16[8,256,256]{2,1,0:T(8,128)(2,1)} %stack.2), calls=%async_computation | async-start | bytes 2097152 | tf_op jit(solution)/shard_map/all_to_all | solution.py:68
  337.2 61.7 %reduce-scatter.7.cloned.1.call-start = ((), (), s32[]{:S(2)}) async-start(), calls=%async_computation.5 | async-start | bytes 147456
  338.1 10.7 %copy-start.7 = (s32[16]{0:T(128)}, s32[16]{0:T(128)S(1)}, u32[]{:S(2)}) copy-start(s32[16]{0:T(128)S(1)} %get-tuple-element.13) | copy-start | bytes 196
  338.1 13.3 %copy-start.3 = (s32[1024]{0:T(1024)}, s32[1024]{0:T(1024)S(1)}, u32[]{:S(2)}) copy-start(s32[1024]{0:T(1024)S(1)} %pad_clamp_fusion.1) | copy-start | bytes 12292
  348.1 0.8 copy-start.1
  351.4 9.7 %copy-start.5 = (f32[64]{0:T(128)S(1)}, f32[64]{0:T(128)}, u32[]{:S(2)}) copy-start(f32[64]{0:T(128)} %copy-done.4) | copy-start | bytes 772
  354.4 8.4 %copy-start.6 = (pred[16]{0:T(512)(128)(4,1)S(1)}, pred[16]{0:T(512)(128)(4,1)}, u32[]{:S(2)}) copy-start(pred[16]{0:T(512)(128)(4,1)} %get-tuple-element.12) | copy-start | bytes 52
  358.4 6.0 copy-start.9
  362.7 323.5 %reduce-scatter.5.cloned.1.call-start = ((), (), s32[]{:S(2)}) async-start(), calls=%async_computation.4 | async-start | bytes 532480 | tf_op jit(solution)/shard_map/reduce_scatter | solution.py:135
Sparse Core Ops, SparseCore 0:
  11.2 94.1 all-gather.1
  362.8 36.0 reduce-scatter.6
  403.4 139.4 reduce-scatter.4
